TPU v7x, 256 devices: a whole 4x4x8 slice. The times are simulated.
256 devices in a mesh: head: 8 (over z), page: 32 (over y, x, core).
Axes of the slice: x: 4, y: 4, z: 8, core: 2. Of those that a mesh axis runs over, the one named last changes fastest.
Arguments:
- doc_states: bfloat16 [2048, 2048], P('page'), may hold values from -6 to 6
- gain_attn: float32 [2048], replicated, may hold values from 0.1 to 1.9
- query_weight: bfloat16 [2048, 2048], P(None, 'head'), may hold values from -0.125 to 0.125
- cache_keys: bfloat16 [64, 128, 2048], P('page', None, 'head'), may hold values from -144 to 144
- cache_values: bfloat16 [64, 128, 2048], P('page', None, 'head'), may hold values from -6 to 6
- rel_bucket: int32 [64, 128], P('page'), may hold values from 0 to 31
- bias_table: float32 [32, 32], P(None, 'head'), may hold values from -4 to 4
- out_weight: bfloat16 [2048, 2048], P('head'), may hold values from -0.125 to 0.125
- gain_ffn: float32 [2048], replicated, may hold values from 0.1 to 1.9
- wi_gate: bfloat16 [2048, 5120], P(None, 'head'), may hold values from -0.125 to 0.125
- wi_up: bfloat16 [2048, 5120], P(None, 'head'), may hold values from -0.125 to 0.125
- wo_ffn: bfloat16 [5120, 2048], P('head'), may hold values from -0.078125 to 0.078125
- score_vector: float32 [2048], replicated, may hold values from -0.125 to 0.125
- query_lengths: int32 [8], replicated, may hold values from 1 to 1024
- doc_query: int32 [256], replicated, may hold values from 0 to 7
- doc_of_token: int32 [2048], replicated, may hold values from 0 to 255, as said below
- page_table: int32 [64], replicated, may hold values from 0 to 63, each once
Outputs:
- doc_scores: float32 [256], P('page')
Inputs may be any that keep to these rules, and one draw needn't show every extreme that they name: page_table lists every physical page once. `doc_of_token`: the tokens of each document form one contiguous run of 1 to 256 tokens; every document has one run, and some document has exactly 256 tokens.
All inputs are finite; a program needn't handle non-finite values.
Results may differ from a plain program's by a relative error of at most 0.03.
Values may be sent and summed in bfloat16 or wider, within the bound.
No kernel may reach another device: no remote copies, remote signals or barrier semaphores. Data moves between devices by JAX's collectives and lax.ppermute only.
A program may use at most 320 MiB of HBM per device.

v0:
```python
import jax
import jax.numpy as jnp
from jax import lax
from jax.sharding import PartitionSpec as P

NQ = 8


def combined_all(value, axis, join):
    pieces = jax.tree.map(lambda part: lax.all_gather(part, axis), value)
    head = jax.tree.map(lambda part: part[0], pieces)
    tail = jax.tree.map(lambda part: part[1:], pieces)
    so_far, _ = lax.scan(lambda so_far, section: (join(so_far, section), None), head, tail)
    return so_far


def rms_scale(values, gain):
    values = values.astype(jnp.float32)
    return values * lax.rsqrt(jnp.mean(values * values, axis=-1, keepdims=True) + 1e-06) * gain


def combine_parts(first, second):
    top_a, total_a, sums_a = first
    top_b, total_b, sums_b = second
    top = jnp.maximum(top_a, top_b)
    scale_a = jnp.exp(top_a - top)
    scale_b = jnp.exp(top_b - top)
    depth = sums_a.shape[1] // top.shape[1]
    sums = sums_a * jnp.repeat(scale_a, depth, axis=1) + sums_b * jnp.repeat(scale_b, depth, axis=1)
    return (top, total_a * scale_a + total_b * scale_b, sums)


def per_device(
    doc_states,
    gain_attn,
    query_weight,
    cache_keys,
    cache_values,
    rel_bucket,
    bias_table,
    out_weight,
    gain_ffn,
    wi_gate,
    wi_up,
    wo_ffn,
    score_vector,
    query_lengths,
    doc_query,
    doc_of_token,
    page_table,
):
    tok_dev = doc_states.shape[0]
    local_pages, page_len, local_width = cache_keys.shape
    local_heads = bias_table.shape[1]
    depth = local_width // local_heads
    key_count = local_pages * page_len
    all_pages = page_table.shape[0]
    max_pages = all_pages // NQ
    page_rank = lax.axis_index("page")
    normed = rms_scale(doc_states, gain_attn).astype(jnp.bfloat16)
    queries = jnp.dot(normed, query_weight, preferred_element_type=jnp.float32).astype(jnp.bfloat16)
    gathered = lax.all_gather(queries, "page", axis=0, tiled=True)
    total_rows = gathered.shape[0]
    doc_ids = jnp.arange(doc_query.shape[0], dtype=jnp.int32)
    tok_query = jnp.sum(
        jnp.where(doc_of_token[:, None] == doc_ids[None, :], doc_query[None, :], 0), axis=1
    )
    page_ids = page_rank * local_pages + jnp.arange(local_pages, dtype=jnp.int32)
    slots = jnp.arange(all_pages, dtype=jnp.int32)
    located = jnp.sum(
        jnp.where(page_table[None, :] == page_ids[:, None], slots[None, :], 0), axis=1
    )
    owner = located // max_pages
    logical = located % max_pages
    query_ids = jnp.arange(NQ, dtype=jnp.int32)
    owner_len = jnp.sum(
        jnp.where(owner[:, None] == query_ids[None, :], query_lengths[None, :], 0), axis=1
    )
    position = logical[:, None] * page_len + jnp.arange(page_len, dtype=jnp.int32)[None, :]
    key_query = jnp.where(position < owner_len[:, None], owner[:, None], -1).reshape(key_count)
    buckets = jnp.arange(bias_table.shape[0], dtype=jnp.int32)
    onehot = (rel_bucket.reshape(key_count)[None, :] == buckets[:, None]).astype(jnp.float32)
    key_bias = jnp.dot(bias_table.T, onehot, precision=lax.Precision.HIGHEST)
    keys = cache_keys.reshape(key_count, local_heads, depth)
    values = cache_values.reshape(key_count, local_heads, depth)
    block = min(512, total_rows)
    count = total_rows // block

    def partial_block(pair):
        rows, owners = pair
        heads = rows.reshape(block, local_heads, depth)
        scores = (
            jnp.einsum("rhd,khd->rhk", heads, keys, preferred_element_type=jnp.float32)
            + key_bias[None]
        )
        mask = (owners[:, None] == key_query[None, :])[:, None, :]
        top = jnp.max(jnp.where(mask, scores, -1e30), axis=-1)
        weights = jnp.where(mask, jnp.exp(scores - top[..., None]), 0.0)
        total = jnp.sum(weights, axis=-1)
        summed = jnp.einsum(
            "rhk,khd->rhd", weights.astype(jnp.bfloat16), values, preferred_element_type=jnp.float32
        )
        return (top, total, summed.reshape(block, local_width))

    tops, totals, summed = lax.map(
        partial_block,
        (gathered.reshape(count, block, local_width), tok_query.reshape(count, block)),
    )
    tops = tops.reshape(total_rows, local_heads)
    totals = totals.reshape(total_rows, local_heads)
    summed = summed.reshape(total_rows, local_width)
    row_start = page_rank * tok_dev
    joined_top, joined_total, joined_sums = combined_all(
        (tops, totals, summed), "page", combine_parts
    )
    own_total = lax.dynamic_slice_in_dim(joined_total, row_start, tok_dev, 0)
    own_sums = lax.dynamic_slice_in_dim(joined_sums, row_start, tok_dev, 0)
    context = (own_sums / jnp.repeat(own_total, depth, axis=1)).astype(jnp.bfloat16)
    projected = lax.psum(
        jnp.dot(context, out_weight, preferred_element_type=jnp.float32).astype(jnp.bfloat16),
        "head",
    ).astype(jnp.float32)
    hidden = doc_states.astype(jnp.float32) + projected
    normed_two = rms_scale(hidden, gain_ffn).astype(jnp.bfloat16)
    gate = jnp.dot(normed_two, wi_gate, preferred_element_type=jnp.float32)
    upper = jnp.dot(normed_two, wi_up, preferred_element_type=jnp.float32)
    middle = (jax.nn.gelu(gate, approximate=True) * upper).astype(jnp.bfloat16)
    ffn_part = jnp.dot(middle, wo_ffn, preferred_element_type=jnp.float32)
    final = hidden + lax.psum(ffn_part.astype(jnp.bfloat16), "head").astype(jnp.float32)
    tok_score = jnp.dot(final, score_vector, precision=lax.Precision.HIGHEST)
    own_docs = lax.dynamic_slice_in_dim(doc_of_token, row_start, tok_dev, 0)
    member = (own_docs[:, None] == doc_ids[None, :]).astype(jnp.float32)
    doc_sums = jnp.dot(tok_score, member, precision=lax.Precision.HIGHEST)
    pooled = lax.psum_scatter(doc_sums, "page", scatter_dimension=0, tiled=True)
    doc_dev = pooled.shape[0]
    mine = page_rank * doc_dev + jnp.arange(doc_dev, dtype=jnp.int32)
    counts = jnp.sum((doc_of_token[:, None] == mine[None, :]).astype(jnp.float32), axis=0)
    return pooled / counts


def solution(mesh):
    return jax.shard_map(
        per_device,
        mesh=mesh,
        in_specs=(
            P("page", None),
            P(),
            P(None, "head"),
            P("page", None, "head"),
            P("page", None, "head"),
            P("page", None),
            P(None, "head"),
            P("head", None),
            P(),
            P(None, "head"),
            P(None, "head"),
            P("head", None),
            P(),
            P(),
            P(),
            P(),
            P(),
        ),
        out_specs=P("page"),
        check_vma=False,
    )
```

profile of v0, /device:TPU:1, one launch (start us, length us, event | category | flops | bytes accessed | tf_op | source)
XLA Modules:
  0.0 1019.1 jit_solution(12967437557516146246)
XLA Ops:
  14.0 48.3 %all-gather.5.cloned.1.call-done = bf16[2048,256]{1,0:T(8,128)(2,1)} async-done(((bf16[64,256]{1,0:T(8,128)(2,1)}), bf16[2048,256]{1,0:T(8,128)(2,1)}) %all-gather.5.cloned.1.call-update) | async-done | bytes 1048592 | tf_op jit(solution)/shard_map/all_gather | solution.py:62
  62.4 41.0 %while.30 = (s32[]{:T(128)}, f32[4,512,4]{1,2,0:T(4,128)}, f32[4,512,4]{1,2,0:T(4,128)}, f32[4,512,256]{2,1,0:T(8,128)}, s32[4,512]{1,0:T(4,128)S(1)}, /*index=5...) while((s32[]{:T(128)}, f32[4,512,4]{1,2,0:T(4,128)}, ...), condition=%wide.region_7.8_spmd.clone, body=%wide.region_4.7_spmd.clone.sunk | while | flops 140112640 | bytes 19551472 | solution.py:105
  104.7 46.0 %all-gather.7.cloned.1.call-done = f32[32,2048,4]{1,2,0:T(4,128)} async-done(((f32[1,2048,4]{1,2,0:T(4,128)}), f32[32,2048,4]{1,2,0:T(4,128)}) %all-gather.7.cloned.1.call-update) | async-done | bytes 1048592 | tf_op jit(solution)/shard_map/all_gather | solution.py:10
  153.0 47.5 %all-gather.9.cloned.1.call-done = f32[32,2048,4]{1,2,0:T(4,128)} async-done(((f32[1,2048,4]{1,2,0:T(4,128)}), f32[32,2048,4]{1,2,0:T(4,128)}) %all-gather.9.cloned.1.call-update) | async-done | bytes 1048592 | tf_op jit(solution)/shard_map/all_gather | solution.py:10
  204.3 204.0 %all-gather.11.cloned.1.call-done = f32[32,2048,256]{2,1,0:T(8,128)} async-done(((f32[1,2048,256]{2,1,0:T(8,128)}), f32[32,2048,256]{2,1,0:T(8,128)}) %all-gather.11.cloned.1.call-update) | async-done | bytes 67108880 | tf_op jit(solution)/shard_map/all_gather | solution.py:10
  414.3 43.9 %slice.29 = f32[31,2048,256]{2,1,0:T(8,128)} slice(f32[32,2048,256]{2,1,0:T(8,128)} %all-gather.11.cloned.1.call-done), slice={[1:32], [0:2048], [0:256]} | slice | bytes 130023424 | tf_op jit(solution)/shard_map/slice | solution.py:12
  458.2 335.9 %while.29 = (s32[]{:T(128)}, f32[2048,4]{0,1:T(4,128)S(1)}, f32[2048,4]{0,1:T(4,128)S(1)}, f32[2048,256]{0,1:T(8,128)}, f32[31,2048,4]{1,2,0:T(4,128)}, /*index=...) while((s32[]{:T(128)}, f32[2048,4]{0,1:T(4,128)S(1)}, f32[2048,4]{0,1:T(4,128)S(1)}, ...), condition=%wide.region_9.10_spmd, body=%wide.region_8.9_spmd.sunk | while | flops 1622018 | bytes 15007837 | solution.py:13
  465.1 4.0 fusion.75
  486.8 4.0 fusion.75
  497.6 4.0 fusion.75
  508.4 4.0 fusion.75
  519.3 4.0 fusion.75
  530.1 4.0 fusion.75
  540.9 4.0 fusion.75
  551.8 4.0 fusion.75
  562.6 4.0 fusion.75
  573.4 4.0 fusion.75
  584.3 4.0 fusion.75
  605.9 4.0 fusion.75
  627.6 4.0 fusion.75
  649.3 4.0 fusion.75
  797.6 66.7 %all-reduce.4.cloned.1.call-done = bf16[64,2048]{1,0:T(8,128)(2,1)} async-done(((bf16[64,2048]{1,0:T(8,128)(2,1)}), bf16[64,2048]{1,0:T(8,128)(2,1)}) %all-reduce.4.cloned.1.call-update) | async-done | bytes 262160 | tf_op jit(solution)/shard_map/psum | solution.py:119
  873.2 69.5 %all-reduce.6.cloned.1.call-done = bf16[64,2048]{1,0:T(8,128)(2,1)} async-done(((bf16[64,2048]{1,0:T(8,128)(2,1)}), bf16[64,2048]{1,0:T(8,128)(2,1)}) %all-reduce.6.cloned.1.call-update) | async-done | bytes 262160 | tf_op jit(solution)/shard_map/psum | solution.py:129
  944.4 67.2 %all-reduce = f32[256]{0:T(256)S(1)} all-reduce(f32[256]{0:T(256)S(1)} %bitcast.123), channel_id=2, replica_groups=mesh['head'=8,'page'=32] {'page'}, use_global_device_ids=true, to_apply=%region_13.14.clone | all-reduce | flops 256 | bytes 2048
  (255 shorter events, 354.6 us)
Async XLA Ops:
  6.5 861.5 %copy-start = (bf16[640,2048]{1,0:T(8,128)(2,1)S(1)}, bf16[640,2048]{1,0:T(8,128)(2,1)}, u32[]{:S(2)}) copy-start(bf16[640,2048]{1,0:T(8,128)(2,1)} %param.32) | copy-start | bytes 7864324
  6.5 4.9 copy-start.4
  6.5 5.1 copy-start.11
  6.5 5.1 copy-start.8
  6.5 5.9 copy-start.14
  6.5 6.6 copy-start.15
  6.6 7.4 copy-start.13
  6.6 7.3 copy-start.12
  6.6 55.8 %all-gather.5.cloned.1.call-start = ((), (), s32[]{:S(2)}) async-start(), calls=%async_computation | async-start | bytes 1081344 | tf_op jit(solution)/shard_map/all_gather | solution.py:62
  10.2 140.5 %all-gather.7.cloned.1.call-start = ((), (), s32[]{:S(2)}) async-start(), calls=%async_computation.1 | async-start | bytes 1081344 | tf_op jit(solution)/shard_map/all_gather | solution.py:10
  69.9 2.8 copy-start.6
  80.1 2.8 copy-start.6
  90.4 2.8 copy-start.6
  100.6 2.8 copy-start.6
  103.4 97.1 %all-gather.9.cloned.1.call-start = ((), (), s32[]{:S(2)}) async-start(), calls=%async_computation.2 | async-start | bytes 1081344 | tf_op jit(solution)/shard_map/all_gather | solution.py:10
  104.1 304.3 %all-gather.11.cloned.1.call-start = ((), (), s32[]{:S(2)}) async-start(), calls=%async_computation.3 | async-start | bytes 69206016 | tf_op jit(solution)/shard_map/all_gather | solution.py:10
  104.7 759.6 %all-reduce.4.cloned.1.call-start = ((), (), s32[]{:S(2)}) async-start(), calls=%async_computation.4 | async-start | bytes 524288 | tf_op jit(solution)/shard_map/psum | solution.py:119
  458.2 406.1 %copy-start.2 = (bf16[64,2048]{1,0:T(8,128)(2,1)S(1)}, bf16[64,2048]{1,0:T(8,128)(2,1)}, u32[]{:S(2)}) copy-start(bf16[64,2048]{1,0:T(8,128)(2,1)} %param.21) | copy-start | bytes 786436
  794.2 71.4 %copy-start.7 = (f32[2048]{0:T(1024)S(1)}, f32[2048]{0:T(1024)}, u32[]{:S(2)}) copy-start(f32[2048]{0:T(1024)} %param.29) | copy-start | bytes 24580
  797.5 145.2 %all-reduce.6.cloned.1.call-start = ((), (), s32[]{:S(2)}) async-start(), calls=%async_computation.5 | async-start | bytes 524288 | tf_op jit(solution)/shard_map/psum | solution.py:129
  864.3 3.7 copy-start.3
  868.0 3.6 copy-start.9
  868.0 3.7 copy-start.16
  868.0 74.7 %copy-start.10 = (f32[2048]{0:T(1024)S(1)}, f32[2048]{0:T(1024)}, u32[]{:S(2)}) copy-start(f32[2048]{0:T(1024)} %param.33) | copy-start | bytes 24580
  (8 other events, 9.1 us)
Sparse Core Ops, SparseCore 0:
  10.3 52.0 all-gather.4
  103.5 47.1 all-gather.6
  153.3 47.1 all-gather.8
  202.9 205.4 all-gather.10
  797.6 66.6 all-reduce.3
  871.8 70.8 all-reduce.5
where the time goes:
time: 1020 us
  waiting for transfers between devices  483 us (47%)
  local copies, waits for them, and re-layouts  264 us (26%)
  other arithmetic  170 us (17%)
  blocking collectives  67.2 us (7%)
  matrix products  20.4 us (2%)
  between operations  14.4 us (1%)
    all_gather x3, waiting for transfers between devices, combined_all(): pieces = jax.tree.map(lambda part: lax.all_gather(part, axis), value)  298 us
    dynamic_slice x62, local copies, waits for them, and re-layouts, combined_all(): lax.scan(lambda so_far, section: (join(so_far, section), None), head, tail)  185 us
    add x31, other arithmetic, combine_parts(): sums_a * jnp.repeat(scale_a, depth, axis=1)  125 us
    psum x1, waiting for transfers between devices, per_device(): lax.psum(ffn_part.astype(jnp.bfloat16), 'head').astype(jnp.float32)  69.5 us
    unnamed x1, blocking collectives  67.2 us
    psum x1, waiting for transfers between devices, per_device(): lax.psum(jnp.dot(context, out_weight, preferred_element_type=jnp.float32)...  66.7 us
    slice x3, local copies, waits for them, and re-layouts, combined_all(): tail = jax.tree.map(lambda part: part[1:], pieces)  48.5 us
    all_gather x1, waiting for transfers between devices, per_device(): gathered = lax.all_gather(queries, 'page', axis=0, tiled=True)  48.3 us
  transfers between devices with their start and end apart: 6, of which 6 were waited for; matrix products, arithmetic and copies ran while one was open for 1% of the time, Pallas kernels for 0%

commit v1 on v0

--- a/solution.py
+++ b/solution.py
@@ -1,9 +1,18 @@
+import functools
 import jax
 import jax.numpy as jnp
 from jax import lax
 from jax.sharding import PartitionSpec as P
 
 NQ = 8
+
+
+def manage_the_tails(field, dev_axis):
+    outcome_arr = lax.all_gather(field, dev_axis)
+    return jnp.sum(outcome_arr, axis=0)
+
+
+forms_group = functools.partial(manage_the_tails, dev_axis="head")
 
 
 def combined_all(value, axis, join):
@@ -126,7 +135,7 @@
     upper = jnp.dot(normed_two, wi_up, preferred_element_type=jnp.float32)
     middle = (jax.nn.gelu(gate, approximate=True) * upper).astype(jnp.bfloat16)
     ffn_part = jnp.dot(middle, wo_ffn, preferred_element_type=jnp.float32)
-    final = hidden + lax.psum(ffn_part.astype(jnp.bfloat16), "head").astype(jnp.float32)
+    final = hidden + forms_group(ffn_part.astype(jnp.bfloat16)).astype(jnp.float32)
     tok_score = jnp.dot(final, score_vector, precision=lax.Precision.HIGHEST)
     own_docs = lax.dynamic_slice_in_dim(doc_of_token, row_start, tok_dev, 0)
     member = (own_docs[:, None] == doc_ids[None, :]).astype(jnp.float32)

time: 1020 us -> 994 us (0.975)
  waiting for transfers between devices: 483 us -> 453 us
    psum x1 -> x0, waiting for transfers between devices: 69.5 us -> none  [per_device(): lax.psum(ffn_part.astype(jnp.bfloat16), 'head').astype(jnp.float32)]
    all_gather x0 -> x1, waiting for transfers between devices: none -> 39 us  [manage_the_tails(): outcome_arr = lax.all_gather(field, dev_axis)]
where the time goes in v1:
time: 994 us; the launch traced here: 989 us
  waiting for transfers between devices  453 us (46%)
  local copies, waits for them, and re-layouts  264 us (27%)
  other arithmetic  172 us (17%)
  blocking collectives  66.4 us (7%)
  matrix products  19.4 us (2%)
  between operations  14.4 us (1%)
    all_gather x3, waiting for transfers between devices, combined_all(): pieces = jax.tree.map(lambda part: lax.all_gather(part, axis), value)  298 us
    dynamic_slice x62, local copies, waits for them, and re-layouts, combined_all(): lax.scan(lambda so_far, section: (join(so_far, section), None), head, tail)  185 us
    add x31, other arithmetic, combine_parts(): sums_a * jnp.repeat(scale_a, depth, axis=1)  125 us
    psum x1, waiting for transfers between devices, per_device(): lax.psum(jnp.dot(context, out_weight, preferred_element_type=jnp.float32)...  66.7 us
    unnamed x1, blocking collectives  66.4 us
    slice x3, local copies, waits for them, and re-layouts, combined_all(): tail = jax.tree.map(lambda part: part[1:], pieces)  48.5 us
    all_gather x1, waiting for transfers between devices, per_device(): gathered = lax.all_gather(queries, 'page', axis=0, tiled=True)  48.3 us
    all_gather x1, waiting for transfers between devices, manage_the_tails(): outcome_arr = lax.all_gather(field, dev_axis)  39 us
  transfers between devices with their start and end apart: 6, of which 6 were waited for; matrix products, arithmetic and copies ran while one was open for 1% of the time, Pallas kernels for 0%

profile of v1, /device:TPU:1, one launch (start us, length us, event | category | flops | bytes accessed | tf_op | source)
XLA Modules:
  0.0 988.8 jit_solution(12342755481087112973)
XLA Ops:
  14.0 48.3 %all-gather.7.cloned.1.call-done = bf16[2048,256]{1,0:T(8,128)(2,1)} async-done(((bf16[64,256]{1,0:T(8,128)(2,1)}), bf16[2048,256]{1,0:T(8,128)(2,1)}) %all-gather.7.cloned.1.call-update) | async-done | bytes 1048592 | tf_op jit(solution)/shard_map/all_gather | solution.py:71
  62.4 41.0 %while.30 = (s32[]{:T(128)}, f32[4,512,4]{1,2,0:T(4,128)}, f32[4,512,4]{1,2,0:T(4,128)}, f32[4,512,256]{2,1,0:T(8,128)}, s32[4,512]{1,0:T(4,128)S(1)}, /*index=5...) while((s32[]{:T(128)}, f32[4,512,4]{1,2,0:T(4,128)}, ...), condition=%wide.region_7.8_spmd.clone, body=%wide.region_4.7_spmd.clone.sunk | while | flops 140112640 | bytes 19551472 | solution.py:114
  104.7 46.0 %all-gather.9.cloned.1.call-done = f32[32,2048,4]{1,2,0:T(4,128)} async-done(((f32[1,2048,4]{1,2,0:T(4,128)}), f32[32,2048,4]{1,2,0:T(4,128)}) %all-gather.9.cloned.1.call-update) | async-done | bytes 1048592 | tf_op jit(solution)/shard_map/all_gather | solution.py:19
  153.0 47.5 %all-gather.11.cloned.1.call-done = f32[32,2048,4]{1,2,0:T(4,128)} async-done(((f32[1,2048,4]{1,2,0:T(4,128)}), f32[32,2048,4]{1,2,0:T(4,128)}) %all-gather.11.cloned.1.call-update) | async-done | bytes 1048592 | tf_op jit(solution)/shard_map/all_gather | solution.py:19
  204.3 204.0 %all-gather.13.cloned.1.call-done = f32[32,2048,256]{2,1,0:T(8,128)} async-done(((f32[1,2048,256]{2,1,0:T(8,128)}), f32[32,2048,256]{2,1,0:T(8,128)}) %all-gather.13.cloned.1.call-update) | async-done | bytes 67108880 | tf_op jit(solution)/shard_map/all_gather | solution.py:19
  414.3 43.9 %slice.29 = f32[31,2048,256]{2,1,0:T(8,128)} slice(f32[32,2048,256]{2,1,0:T(8,128)} %all-gather.13.cloned.1.call-done), slice={[1:32], [0:2048], [0:256]} | slice | bytes 130023424 | tf_op jit(solution)/shard_map/slice | solution.py:21
  458.2 335.9 %while.29 = (s32[]{:T(128)}, f32[2048,4]{0,1:T(4,128)S(1)}, f32[2048,4]{0,1:T(4,128)S(1)}, f32[2048,256]{0,1:T(8,128)}, f32[31,2048,4]{1,2,0:T(4,128)}, /*index=...) while((s32[]{:T(128)}, f32[2048,4]{0,1:T(4,128)S(1)}, f32[2048,4]{0,1:T(4,128)S(1)}, ...), condition=%wide.region_9.10_spmd, body=%wide.region_8.9_spmd.sunk | while | flops 1622018 | bytes 15007837 | solution.py:22
  465.1 4.0 fusion.75
  486.8 4.0 fusion.75
  497.6 4.0 fusion.75
  508.4 4.0 fusion.75
  519.3 4.0 fusion.75
  530.1 4.0 fusion.75
  540.9 4.0 fusion.75
  551.8 4.0 fusion.75
  562.6 4.0 fusion.75
  573.4 4.0 fusion.75
  584.3 4.0 fusion.75
  605.9 4.0 fusion.75
  627.6 4.0 fusion.75
  649.3 4.0 fusion.75
  797.6 66.7 %all-reduce.3.cloned.1.call-done = bf16[64,2048]{1,0:T(8,128)(2,1)} async-done(((bf16[64,2048]{1,0:T(8,128)(2,1)}), bf16[64,2048]{1,0:T(8,128)(2,1)}) %all-reduce.3.cloned.1.call-update) | async-done | bytes 262160 | tf_op jit(solution)/shard_map/psum | solution.py:128
  873.2 39.0 %all-gather.15.cloned.1.call-done = bf16[512,2048]{1,0:T(8,128)(2,1)} async-done(((bf16[64,2048]{1,0:T(8,128)(2,1)}), bf16[512,2048]{1,0:T(8,128)(2,1)}) %all-gather.15.cloned.1.call-update) | async-done | bytes 2097168 | tf_op jit(solution)/shard_map/all_gather | solution.py:11
  914.9 66.4 %all-reduce = f32[256]{0:T(256)S(1)} all-reduce(f32[256]{0:T(256)S(1)} %bitcast.125), channel_id=3, replica_groups=mesh['head'=8,'page'=32] {'page'}, use_global_device_ids=true, to_apply=%region_13.14.clone | all-reduce | flops 256 | bytes 2048
  (256 shorter events, 355.6 us)
Async XLA Ops:
  6.5 861.5 %copy-start = (bf16[640,2048]{1,0:T(8,128)(2,1)S(1)}, bf16[640,2048]{1,0:T(8,128)(2,1)}, u32[]{:S(2)}) copy-start(bf16[640,2048]{1,0:T(8,128)(2,1)} %param.32) | copy-start | bytes 7864324
  6.5 4.9 copy-start.4
  6.5 5.1 copy-start.11
  6.5 5.1 copy-start.8
  6.5 5.9 copy-start.14
  6.5 6.6 copy-start.15
  6.6 7.4 copy-start.13
  6.6 7.3 copy-start.12
  6.6 55.8 %all-gather.7.cloned.1.call-start = ((), (), s32[]{:S(2)}) async-start(), calls=%async_computation | async-start | bytes 1081344 | tf_op jit(solution)/shard_map/all_gather | solution.py:71
  10.2 140.5 %all-gather.9.cloned.1.call-start = ((), (), s32[]{:S(2)}) async-start(), calls=%async_computation.1 | async-start | bytes 1081344 | tf_op jit(solution)/shard_map/all_gather | solution.py:19
  69.9 2.8 copy-start.6
  80.1 2.8 copy-start.6
  90.4 2.8 copy-start.6
  100.6 2.8 copy-start.6
  103.4 97.1 %all-gather.11.cloned.1.call-start = ((), (), s32[]{:S(2)}) async-start(), calls=%async_computation.2 | async-start | bytes 1081344 | tf_op jit(solution)/shard_map/all_gather | solution.py:19
  104.1 304.3 %all-gather.13.cloned.1.call-start = ((), (), s32[]{:S(2)}) async-start(), calls=%async_computation.3 | async-start | bytes 69206016 | tf_op jit(solution)/shard_map/all_gather | solution.py:19
  104.7 759.6 %all-reduce.3.cloned.1.call-start = ((), (), s32[]{:S(2)}) async-start(), calls=%async_computation.4 | async-start | bytes 524288 | tf_op jit(solution)/shard_map/psum | solution.py:128
  458.2 406.1 %copy-start.2 = (bf16[64,2048]{1,0:T(8,128)(2,1)S(1)}, bf16[64,2048]{1,0:T(8,128)(2,1)}, u32[]{:S(2)}) copy-start(bf16[64,2048]{1,0:T(8,128)(2,1)} %param.21) | copy-start | bytes 786436
  794.2 71.4 %copy-start.7 = (f32[2048]{0:T(1024)S(1)}, f32[2048]{0:T(1024)}, u32[]{:S(2)}) copy-start(f32[2048]{0:T(1024)} %param.29) | copy-start | bytes 24580
  797.5 114.6 %all-gather.15.cloned.1.call-start = ((), (), s32[]{:S(2)}) async-start(), calls=%async_computation.5 | async-start | bytes 2359296 | tf_op jit(solution)/shard_map/all_gather | solution.py:11
  864.3 3.7 copy-start.3
  868.0 3.6 copy-start.9
  868.0 3.7 copy-start.16
  871.6 42.5 %copy-start.10 = (f32[2048]{0:T(1024)S(1)}, f32[2048]{0:T(1024)}, u32[]{:S(2)}) copy-start(f32[2048]{0:T(1024)} %param.33) | copy-start | bytes 24580
  (8 other events, 9.1 us)
Sparse Core Ops, SparseCore 0:
  10.3 52.0 all-gather.6
  103.5 47.1 all-gather.8
  153.3 47.1 all-gather.10
  202.9 205.4 all-gather.12
  797.6 66.6 all-reduce.2
  871.8 40.3 all-gather.14
